TPU v7x, 512 devices: a whole 4x8x8 slice. The times are simulated.
512 devices in a mesh: row: 16 (over y, core), col: 8 (over z), fib: 4 (over x).
Axes of the slice: x: 4, y: 8, z: 8, core: 2. Of those that a mesh axis runs over, the one named last changes fastest.
Arguments:
- values: bfloat16 [768, 12, 128, 128], P(('row', 'col'), 'fib'), may hold values from -3 to 3
- columns: int32 [768, 12], P(('row', 'col')), may hold values from 0 to 767, as said below
- counts: int32 [768], P(('row', 'col')), may hold values from 6 to 12, as said below
Outputs:
- square: bfloat16 [768, 12, 128, 128], P(('row', 'col'), 'fib')
- traces: float32 [2], replicated
Inputs may be any that keep to these rules, and one draw needn't show every extreme that they name: Slot 0 of block row i holds i. Every slot s >= 1 of row i, used or not, holds (i + o) mod 768 with 1 <= |o| <= 6, and the columns of one row are distinct. Row i uses slots 0 to counts[i] - 1; later slots are ignored. Some row uses all 12 slots.
All inputs are finite; a program needn't handle non-finite values.
Results may differ from a plain program's by a relative error of at most 0.001.
Values may be sent and summed in bfloat16 or wider, within the bound.
A program may use at most 128 MiB of HBM per device.

v0:
```python
import jax
import jax.numpy as jnp
from jax import lax
from jax.sharding import PartitionSpec as P

BAND = 6


def padded(array, sides, width):
    for axis, dim in sides:
        size, length = (lax.axis_size(axis), array.shape[dim])
        up = [(i, (i + 1) % size) for i in range(size)]
        down = [(j, i) for i, j in up]
        last = lax.slice_in_dim(array, length - width, length, axis=dim)
        initial = lax.slice_in_dim(array, 0, width, axis=dim)
        before = lax.ppermute(last, axis, up)
        after = lax.ppermute(initial, axis, down)
        array = jnp.concatenate([before, array, after], axis=dim)
    return array


def band_product(
    left_tiles, left_keep, fetch_index, target_cols, target_keep, window, window_cols, window_counts
):
    picked = jnp.take(window, fetch_index, axis=0)
    picked_cols = jnp.take(window_cols, fetch_index, axis=0)
    picked_counts = jnp.take(window_counts, fetch_index, axis=0)
    alive_slots = lax.broadcasted_iota(jnp.int32, picked_cols.shape, 1) < picked_counts[:, None]
    matches = (picked_cols[:, None, :] == target_cols[None, :, None]) & alive_slots[:, None, :]
    matches = matches & left_keep[:, None, None] & target_keep[None, :, None]
    chosen = jnp.einsum(
        "ajs,asxy->ajxy", matches.astype(jnp.bfloat16), picked, preferred_element_type=jnp.float32
    ).astype(jnp.bfloat16)
    return jnp.einsum("axy,ajyz->jxz", left_tiles, chosen, preferred_element_type=jnp.float32)


def body(values, columns, counts):
    rows_here = values.shape[0]
    share_count = values.shape[1]
    slot_count = columns.shape[1]
    block_total = rows_here * lax.axis_size(("row", "col"))
    fib_index = lax.axis_index("fib")
    full_rows = lax.all_gather(values, "fib", axis=1, tiled=True)
    window, window_cols, window_counts = (
        padded(full_rows, ((("row", "col"), 0),), BAND),
        padded(columns, ((("row", "col"), 0),), BAND),
        padded(counts, ((("row", "col"), 0),), BAND),
    )
    local_rows = jnp.arange(rows_here, dtype=jnp.int32)
    row_ids = lax.axis_index(("row", "col")) * rows_here + local_rows
    fetch_all = (columns - row_ids[:, None] + BAND) % block_total + local_rows[:, None]
    slot_ids = jnp.arange(slot_count, dtype=jnp.int32)
    keep_mask = slot_ids[None, :] < counts[:, None]
    first_slot = fib_index * share_count

    def one_row(operands):
        left_tiles, left_keep, fetch_index, target_cols, target_keep = operands
        return band_product(
            left_tiles,
            left_keep,
            fetch_index,
            target_cols,
            target_keep,
            window,
            window_cols,
            window_counts,
        )

    left_fetch = lax.dynamic_slice_in_dim(fetch_all, first_slot, share_count, 1)
    left_keep = lax.dynamic_slice_in_dim(keep_mask, first_slot, share_count, 1)
    partial_value = lax.map(one_row, (values, left_keep, left_fetch, columns, keep_mask))
    regrouped = lax.all_to_all(partial_value[None], "fib", split_axis=2, concat_axis=0, tiled=True)
    product = jnp.sum(regrouped, axis=0)
    is_first = (fib_index == 0).astype(jnp.float32)
    trace_values = is_first * jnp.sum(
        jnp.diagonal(values[:, 0].astype(jnp.float32), axis1=1, axis2=2)
    )
    trace_square = is_first * jnp.sum(jnp.diagonal(product[:, 0], axis1=1, axis2=2))
    traces = lax.psum(jnp.stack([trace_values, trace_square]), ("row", "col", "fib"))
    return (product.astype(jnp.bfloat16), traces)


def solution(mesh):
    in_specs = (P(("row", "col"), "fib", None, None), P(("row", "col"), None), P(("row", "col")))
    out_specs = (P(("row", "col"), "fib", None, None), P())
    return jax.shard_map(body, mesh=mesh, in_specs=in_specs, out_specs=out_specs, check_vma=False)
```

profile of v0, /device:TPU:1, one launch (start us, length us, event | category | flops | bytes accessed | tf_op | source)
XLA Modules:
  0.0 354.2 jit_solution(3832877042432415155)
XLA Ops:
  7.9 45.8 %all-gather.2.cloned.1.call-done = bf16[6,12,128,128]{3,2,1,0:T(8,128)(2,1)} async-done(((bf16[6,3,128,128]{3,2,1,0:T(8,128)(2,1)}), bf16[6,12,128,128]{3,2,1,0:T(8,128)(2,1)}) %all-gather.2.cloned.1.call-update) | async-done | bytes 2359312 | tf_op jit(solution)/shard_map/all_gather | solution.py:43
  53.7 3.3 collective-permute-start.4
  57.0 5.0 %collective-permute-start.5 = (bf16[6,12,128,128]{3,2,1,0:T(8,128)(2,1)}, bf16[6,12,128,128]{3,2,1,0:T(8,128)(2,1)}, u32[]{:S(2)}, u32[]{:S(2)}) collective-permute-start(bf16[6,12,128,128]{3,2,1,0:T(8,128)(2,1)} %all-gather.2.cloned.1.call-done), channel_id=1, source_target_pairs={{4,0},{8,4},{12,8},{16,12},{20,16},{24,20},{28,24},{32,28},{36,32}... | collective-permute-start | bytes 7077896 | tf_op jit(solution)/shard_map/ppermute | solution.py:17
  61.9 1.9 collective-permute-start
  63.8 4.9 %collective-permute-start.1 = (s32[6,12]{1,0:T(8,128)}, s32[6,12]{1,0:T(8,128)S(1)}, u32[]{:S(2)}, u32[]{:S(2)}) collective-permute-start(s32[6,12]{1,0:T(8,128)} %param.6), channel_id=1, source_target_pairs={{4,0},{8,4},{12,8},{16,12},{20,16},{24,20},{28,24},{32,28},{36,32}... | collective-permute-start | bytes 872 | tf_op jit(solution)/shard_map/ppermute | solution.py:17
  68.7 1.9 collective-permute-start.2
  72.3 39.8 %collective-permute-done.2 = s32[6]{0:T(128)S(1)} collective-permute-done((s32[6]{0:T(128)}, s32[6]{0:T(128)S(1)}, u32[]{:S(2)}, u32[]{:S(2)}) %collective-permute-start.2) | collective-permute-done | bytes 56 | tf_op jit(solution)/shard_map/ppermute | solution.py:16
  112.2 2.9 collective-permute-start.3
  115.1 1.5 collective-permute-done.3
  118.1 5.9 %pad_maximum_fusion = bf16[18,12,128,128]{3,2,1,0:T(8,128)(2,1)} fusion(bf16[6,12,128,128]{3,2,1,0:T(8,128)(2,1)} %collective-permute-done.5, bf16[6,12,128,128]{3,2,1,0:T(8,128)(2,1)} %all-gather.2.cloned.1.call-done, bf16[6,12,128,128]{3,2,1,0:T(8,128)(2,1)S(1)} %collective-permute-done.4), kind=kLoop, calls=%fused_computation.37 | loop fusion | flops 7077888 | bytes 14155776 | tf_op jit(solution)/shard_map/concatenate | solution.py:18
  123.9 50.9 %while.10 = (s32[]{:T(128)}, f32[6,12,128,128]{2,3,0,1:T(8,128)}, s32[6,3]{1,0:T(8,128)S(1)}, s32[18,12]{1,0:T(8,128)S(1)}, s32[6,12]{1,0:T(8,128)}, /*index=5*/...) while((s32[]{:T(128)}, f32[6,12,128,128]{2,3,0,1:T(8,128)}, ...), condition=%wide.region_1.2_spmd, body=%wide.region_0.1_spmd.sunk | while | flops 166333216 | bytes 9541871 | solution.py:71
  124.6 3.8 %gather_fusion = bf16[3,12,128,128]{3,2,1,0:T(8,128)(2,1)S(1)} fusion(bf16[18,12,128,128]{3,2,1,0:T(8,128)(2,1)} %get-tuple-element.178, s32[1024]{0:T(1024)S(1)} %pad_clamp_fusion.2), kind=kCustom, calls=%fused_computation.2.clone.1 | custom fusion | bytes 2359308 | tf_op jit(solution)/shard_map/while/body/eval_jaxpr/jit(_take)/gather | solution.py:25
  131.0 1.5 fusion.32
  133.1 3.8 %gather_fusion = bf16[3,12,128,128]{3,2,1,0:T(8,128)(2,1)S(1)} fusion(bf16[18,12,128,128]{3,2,1,0:T(8,128)(2,1)} %get-tuple-element.178, s32[1024]{0:T(1024)S(1)} %pad_clamp_fusion.2), kind=kCustom, calls=%fused_computation.2.clone.1 | custom fusion | bytes 2359308 | tf_op jit(solution)/shard_map/while/body/eval_jaxpr/jit(_take)/gather | solution.py:25
  139.4 1.5 fusion.32
  141.6 3.8 %gather_fusion = bf16[3,12,128,128]{3,2,1,0:T(8,128)(2,1)S(1)} fusion(bf16[18,12,128,128]{3,2,1,0:T(8,128)(2,1)} %get-tuple-element.178, s32[1024]{0:T(1024)S(1)} %pad_clamp_fusion.2), kind=kCustom, calls=%fused_computation.2.clone.1 | custom fusion | bytes 2359308 | tf_op jit(solution)/shard_map/while/body/eval_jaxpr/jit(_take)/gather | solution.py:25
  147.9 1.5 fusion.32
  150.1 3.8 %gather_fusion = bf16[3,12,128,128]{3,2,1,0:T(8,128)(2,1)S(1)} fusion(bf16[18,12,128,128]{3,2,1,0:T(8,128)(2,1)} %get-tuple-element.178, s32[1024]{0:T(1024)S(1)} %pad_clamp_fusion.2), kind=kCustom, calls=%fused_computation.2.clone.1 | custom fusion | bytes 2359308 | tf_op jit(solution)/shard_map/while/body/eval_jaxpr/jit(_take)/gather | solution.py:25
  156.4 1.5 fusion.32
  158.5 3.8 %gather_fusion = bf16[3,12,128,128]{3,2,1,0:T(8,128)(2,1)S(1)} fusion(bf16[18,12,128,128]{3,2,1,0:T(8,128)(2,1)} %get-tuple-element.178, s32[1024]{0:T(1024)S(1)} %pad_clamp_fusion.2), kind=kCustom, calls=%fused_computation.2.clone.1 | custom fusion | bytes 2359308 | tf_op jit(solution)/shard_map/while/body/eval_jaxpr/jit(_take)/gather | solution.py:25
  164.9 1.5 fusion.32
  167.0 3.8 %gather_fusion = bf16[3,12,128,128]{3,2,1,0:T(8,128)(2,1)S(1)} fusion(bf16[18,12,128,128]{3,2,1,0:T(8,128)(2,1)} %get-tuple-element.178, s32[1024]{0:T(1024)S(1)} %pad_clamp_fusion.2), kind=kCustom, calls=%fused_computation.2.clone.1 | custom fusion | bytes 2359308 | tf_op jit(solution)/shard_map/while/body/eval_jaxpr/jit(_take)/gather | solution.py:25
  173.3 1.5 fusion.32
  174.8 5.0 %all-to-all-start = ((f32[1,6,12,128,128]{3,4,1,0,2:T(8,128)}), f32[1,6,12,128,128]{3,4,1,0,2:T(8,128)}, u32[]{:S(2)}, u32[]{:S(2)}) async-start(f32[1,6,12,128,128]{3,4,1,0,2:T(8,128)} %bitcast.60), calls=%async_computation | async-start | bytes 9437184 | tf_op jit(solution)/shard_map/all_to_all | solution.py:72
  179.9 3.3 copy.13
  183.2 6.5 %bitcast_convert_fusion = f32[6,128,128]{0,2,1:T(8,128)} fusion(bf16[6,1,128,128]{0,3,2,1:T(8,128)(2,1)} %copy.13), kind=kLoop, calls=%fused_computation.38 | loop fusion | flops 98304 | bytes 589824 | tf_op jit(solution)/shard_map/convert_element_type | solution.py:76
  189.7 1.8 gather_fusion.3
  192.7 40.7 %all-to-all-done = f32[1,6,12,128,128]{3,4,1,0,2:T(8,128)} async-done(((f32[1,6,12,128,128]{3,4,1,0,2:T(8,128)}), f32[1,6,12,128,128]{3,4,1,0,2:T(8,128)}, u32[]{:S(2)}, u32[]{:S(2)}) %all-to-all-start) | async-done | bytes 4718624 | tf_op jit(solution)/shard_map/all_to_all | solution.py:72
  233.4 2.9 reduce_sum.27
  236.4 7.6 %copy.21 = f32[6,1,128,128]{0,3,2,1:T(8,128)} copy(f32[6,1,128,128]{2,3,1,0:T(8,128)S(1)} %copy.33) | data formatting | bytes 786432
  244.0 1.8 gather_fusion.4
  247.2 99.0 %psum.7 = f32[2]{0:T(128)} all-reduce(f32[2]{0:T(128)S(1)} %pad_maximum_fusion.1), channel_id=1, replica_groups=mesh['row'=16,'col'=8,'fib'=4] {'row','col','fib'}, use_global_device_ids=true, to_apply=%region_5.6 | all-reduce | flops 2 | bytes 16 | tf_op jit(solution)/shard_map/psum | solution.py:79
  (97 shorter events, 25.5 us)
Async XLA Ops:
  7.2 46.5 %all-gather.2.cloned.1.call-start = ((), (), s32[]{:S(2)}) async-start(), calls=%async_computation.1 | async-start | bytes 2949120 | tf_op jit(solution)/shard_map/all_gather | solution.py:43
  53.7 64.4 %collective-permute-start.4 = (bf16[6,12,128,128]{3,2,1,0:T(8,128)(2,1)}, bf16[6,12,128,128]{3,2,1,0:T(8,128)(2,1)S(1)}, u32[]{:S(2)}, u32[]{:S(2)}) collective-permute-start(bf16[6,12,128,128]{3,2,1,0:T(8,128)(2,1)} %all-gather.2.cloned.1.call-done), channel_id=1, source_target_pairs={{0,4},{4,8},{8,12},{12,16},{16,20},{20,24},{24,28},{28,32},{32,36}... | collective-permute-start | bytes 7077896 | tf_op jit(solution)/shard_map/ppermute | solution.py:16
  57.0 61.1 %collective-permute-start.5 = (bf16[6,12,128,128]{3,2,1,0:T(8,128)(2,1)}, bf16[6,12,128,128]{3,2,1,0:T(8,128)(2,1)}, u32[]{:S(2)}, u32[]{:S(2)}) collective-permute-start(bf16[6,12,128,128]{3,2,1,0:T(8,128)(2,1)} %all-gather.2.cloned.1.call-done), channel_id=1, source_target_pairs={{4,0},{8,4},{12,8},{16,12},{20,16},{24,20},{28,24},{32,28},{36,32}... | collective-permute-start | bytes 7077896 | tf_op jit(solution)/shard_map/ppermute | solution.py:17
  61.9 55.4 %collective-permute-start = (s32[6,12]{1,0:T(8,128)}, s32[6,12]{1,0:T(8,128)S(1)}, u32[]{:S(2)}, u32[]{:S(2)}) collective-permute-start(s32[6,12]{1,0:T(8,128)} %param.6), channel_id=1, source_target_pairs={{0,4},{4,8},{8,12},{12,16},{16,20},{20,24},{24,28},{28,32},{32,36}... | collective-permute-start | bytes 872 | tf_op jit(solution)/shard_map/ppermute | solution.py:16
  63.8 53.5 %collective-permute-start.1 = (s32[6,12]{1,0:T(8,128)}, s32[6,12]{1,0:T(8,128)S(1)}, u32[]{:S(2)}, u32[]{:S(2)}) collective-permute-start(s32[6,12]{1,0:T(8,128)} %param.6), channel_id=1, source_target_pairs={{4,0},{8,4},{12,8},{16,12},{20,16},{24,20},{28,24},{32,28},{36,32}... | collective-permute-start | bytes 872 | tf_op jit(solution)/shard_map/ppermute | solution.py:17
  68.7 43.5 %collective-permute-start.2 = (s32[6]{0:T(128)}, s32[6]{0:T(128)S(1)}, u32[]{:S(2)}, u32[]{:S(2)}) collective-permute-start(s32[6]{0:T(128)} %param.7), channel_id=1, source_target_pairs={{0,4},{4,8},{8,12},{12,16},{16,20},{20,24},{24,28},{28,32},{32,36}... | collective-permute-start | bytes 80 | tf_op jit(solution)/shard_map/ppermute | solution.py:16
  112.2 4.4 %collective-permute-start.3 = (s32[6]{0:T(128)}, s32[6]{0:T(128)S(1)}, u32[]{:S(2)}, u32[]{:S(2)}) collective-permute-start(s32[6]{0:T(128)} %param.7), channel_id=1, source_target_pairs={{4,0},{8,4},{12,8},{16,12},{20,16},{24,20},{28,24},{32,28},{36,32}... | collective-permute-start | bytes 80 | tf_op jit(solution)/shard_map/ppermute | solution.py:17
  118.0 5.9 %copy-start = (bf16[6,3,128,128]{3,2,1,0:T(8,128)(2,1)S(1)}, bf16[6,3,128,128]{3,2,1,0:T(8,128)(2,1)}, u32[]{:S(2)}) copy-start(bf16[6,3,128,128]{3,2,1,0:T(8,128)(2,1)} %param.5) | copy-start | bytes 1769476
  174.8 58.6 %all-to-all-start = ((f32[1,6,12,128,128]{3,4,1,0,2:T(8,128)}), f32[1,6,12,128,128]{3,4,1,0,2:T(8,128)}, u32[]{:S(2)}, u32[]{:S(2)}) async-start(f32[1,6,12,128,128]{3,4,1,0,2:T(8,128)} %bitcast.60), calls=%async_computation | async-start | bytes 9437184 | tf_op jit(solution)/shard_map/all_to_all | solution.py:72
Sparse Core Ops, SparseCore 0:
  10.1 43.5 all-gather.1
where the time goes:
time: 355 us; the launch traced here: 354 us
  waiting for transfers between devices  129 us (36%)
  blocking collectives  99 us (28%)
  local copies, waits for them, and re-layouts  50 us (14%)
  starting transfers between devices  24.9 us (7%)
  other arithmetic  21.6 us (6%)
  between operations  15.5 us (4%)
  matrix products  14.4 us (4%)
    psum x1, blocking collectives, body(): lax.psum(jnp.stack([trace_values, trace_square]), ('row', 'col', 'fib'))  99 us
    all_gather x1, waiting for transfers between devices, body(): full_rows = lax.all_gather(values, 'fib', axis=1, tiled=True)  45.8 us
    all_to_all x1, waiting for transfers between devices, body(): lax.all_to_all(partial_value[None], 'fib', split_axis=2, concat_axis=0, t...  40.7 us
    ppermute x3, waiting for transfers between devices, padded(): before = lax.ppermute(last, axis, up)  39.8 us
    gather x6, local copies, waits for them, and re-layouts, band_product(): picked = jnp.take(window, fetch_index, axis=0)  22.7 us
    ppermute x3, starting transfers between devices, padded(): after = lax.ppermute(initial, axis, down)  12.7 us
    dot_general x6, matrix products, band_product(): jnp.einsum('axy,ajyz->jxz', left_tiles, chosen, preferred_element_type=jn...  8.83 us
    unnamed x6, local copies, waits for them, and re-layouts  8.81 us
  transfers between devices with their start and end apart: 8, of which 4 were waited for; matrix products, arithmetic and copies ran while one was open for 4% of the time, Pallas kernels for 0%

commit v1 on v0

--- a/solution.py
+++ b/solution.py
@@ -76,7 +76,9 @@
         jnp.diagonal(values[:, 0].astype(jnp.float32), axis1=1, axis2=2)
     )
     trace_square = is_first * jnp.sum(jnp.diagonal(product[:, 0], axis1=1, axis2=2))
-    traces = lax.psum(jnp.stack([trace_values, trace_square]), ("row", "col", "fib"))
+    traces = jnp.stack([trace_values, trace_square])
+    for over in ("row", ("col", "fib")):
+        traces = lax.psum(traces, over)
     return (product.astype(jnp.bfloat16), traces)
 
 

time: 355 us -> 354 us (level)
  the two profiles are of different devices: /device:TPU:1 before, /device:TPU:32 now
where the time goes in v1:
time: 354 us; the launch traced here: 353 us
  waiting for transfers between devices  122 us (34%)
  blocking collectives  99.8 us (28%)
  local copies, waits for them, and re-layouts  50 us (14%)
  starting transfers between devices  29.9 us (8%)
  other arithmetic  21.7 us (6%)
  between operations  15.5 us (4%)
  matrix products  14.3 us (4%)
    psum x2, blocking collectives, body(): traces = lax.psum(traces, over)  99.8 us
    all_gather x1, waiting for transfers between devices, body(): full_rows = lax.all_gather(values, 'fib', axis=1, tiled=True)  44.8 us
    all_to_all x1, waiting for transfers between devices, body(): lax.all_to_all(partial_value[None], 'fib', split_axis=2, concat_axis=0, t...  42.2 us
    ppermute x3, waiting for transfers between devices, padded(): before = lax.ppermute(last, axis, up)  32.8 us
    gather x6, local copies, waits for them, and re-layouts, band_product(): picked = jnp.take(window, fetch_index, axis=0)  22.7 us
    ppermute x3, starting transfers between devices, padded(): after = lax.ppermute(initial, axis, down)  17.4 us
    unnamed x6, local copies, waits for them, and re-layouts  8.77 us
    dot_general x6, matrix products, band_product(): jnp.einsum('axy,ajyz->jxz', left_tiles, chosen, preferred_element_type=jn...  8.71 us
  transfers between devices with their start and end apart: 8, of which 4 were waited for; matrix products, arithmetic and copies ran while one was open for 4% of the time, Pallas kernels for 0%

profile of v1, /device:TPU:32, one launch (start us, length us, event | category | flops | bytes accessed | tf_op | source)
XLA Modules:
  0.0 353.1 jit_solution(3038775738257660710)
XLA Ops:
  7.9 44.8 %all-gather.2.cloned.1.call-done = bf16[6,12,128,128]{3,2,1,0:T(8,128)(2,1)} async-done(((bf16[6,3,128,128]{3,2,1,0:T(8,128)(2,1)}), bf16[6,12,128,128]{3,2,1,0:T(8,128)(2,1)}) %all-gather.2.cloned.1.call-update) | async-done | bytes 2359312 | tf_op jit(solution)/shard_map/all_gather | solution.py:43
  52.7 3.5 %collective-permute-start.4 = (bf16[6,12,128,128]{3,2,1,0:T(8,128)(2,1)}, bf16[6,12,128,128]{3,2,1,0:T(8,128)(2,1)S(1)}, u32[]{:S(2)}, u32[]{:S(2)}) collective-permute-start(bf16[6,12,128,128]{3,2,1,0:T(8,128)(2,1)} %all-gather.2.cloned.1.call-done), channel_id=1, source_target_pairs={{0,4},{4,8},{8,12},{12,16},{16,20},{20,24},{24,28},{28,32},{32,36}... | collective-permute-start | bytes 7077896 | tf_op jit(solution)/shard_map/ppermute | solution.py:16
  56.2 5.3 %collective-permute-start.5 = (bf16[6,12,128,128]{3,2,1,0:T(8,128)(2,1)}, bf16[6,12,128,128]{3,2,1,0:T(8,128)(2,1)}, u32[]{:S(2)}, u32[]{:S(2)}) collective-permute-start(bf16[6,12,128,128]{3,2,1,0:T(8,128)(2,1)} %all-gather.2.cloned.1.call-done), channel_id=1, source_target_pairs={{4,0},{8,4},{12,8},{16,12},{20,16},{24,20},{28,24},{32,28},{36,32}... | collective-permute-start | bytes 7077896 | tf_op jit(solution)/shard_map/ppermute | solution.py:17
  61.6 1.9 collective-permute-start
  63.5 7.0 %collective-permute-start.1 = (s32[6,12]{1,0:T(8,128)}, s32[6,12]{1,0:T(8,128)S(1)}, u32[]{:S(2)}, u32[]{:S(2)}) collective-permute-start(s32[6,12]{1,0:T(8,128)} %param.6), channel_id=1, source_target_pairs={{4,0},{8,4},{12,8},{16,12},{20,16},{24,20},{28,24},{32,28},{36,32}... | collective-permute-start | bytes 872 | tf_op jit(solution)/shard_map/ppermute | solution.py:17
  70.5 1.9 collective-permute-start.2
  74.1 32.8 %collective-permute-done.2 = s32[6]{0:T(128)S(1)} collective-permute-done((s32[6]{0:T(128)}, s32[6]{0:T(128)S(1)}, u32[]{:S(2)}, u32[]{:S(2)}) %collective-permute-start.2) | collective-permute-done | bytes 56 | tf_op jit(solution)/shard_map/ppermute | solution.py:16
  106.9 5.1 %collective-permute-start.3 = (s32[6]{0:T(128)}, s32[6]{0:T(128)S(1)}, u32[]{:S(2)}, u32[]{:S(2)}) collective-permute-start(s32[6]{0:T(128)} %param.7), channel_id=1, source_target_pairs={{4,0},{8,4},{12,8},{16,12},{20,16},{24,20},{28,24},{32,28},{36,32}... | collective-permute-start | bytes 80 | tf_op jit(solution)/shard_map/ppermute | solution.py:17
  114.9 5.9 %pad_maximum_fusion = bf16[18,12,128,128]{3,2,1,0:T(8,128)(2,1)} fusion(bf16[6,12,128,128]{3,2,1,0:T(8,128)(2,1)} %collective-permute-done.5, bf16[6,12,128,128]{3,2,1,0:T(8,128)(2,1)} %all-gather.2.cloned.1.call-done, bf16[6,12,128,128]{3,2,1,0:T(8,128)(2,1)S(1)} %collective-permute-done.4), kind=kLoop, calls=%fused_computation.37 | loop fusion | flops 7077888 | bytes 14155776 | tf_op jit(solution)/shard_map/concatenate | solution.py:18
  120.8 50.7 %while.10 = (s32[]{:T(128)}, f32[6,12,128,128]{2,3,0,1:T(8,128)}, s32[6,3]{1,0:T(8,128)S(1)}, s32[18,12]{1,0:T(8,128)S(1)}, s32[6,12]{1,0:T(8,128)}, /*index=5*/...) while((s32[]{:T(128)}, f32[6,12,128,128]{2,3,0,1:T(8,128)}, ...), condition=%wide.region_1.2_spmd, body=%wide.region_0.1_spmd.sunk | while | flops 166333216 | bytes 9541871 | solution.py:71
  121.5 3.8 %gather_fusion = bf16[3,12,128,128]{3,2,1,0:T(8,128)(2,1)S(1)} fusion(bf16[18,12,128,128]{3,2,1,0:T(8,128)(2,1)} %get-tuple-element.178, s32[1024]{0:T(1024)S(1)} %pad_clamp_fusion.2), kind=kCustom, calls=%fused_computation.2.clone.1 | custom fusion | bytes 2359308 | tf_op jit(solution)/shard_map/while/body/eval_jaxpr/jit(_take)/gather | solution.py:25
  127.8 1.5 fusion.32
  130.0 3.8 %gather_fusion = bf16[3,12,128,128]{3,2,1,0:T(8,128)(2,1)S(1)} fusion(bf16[18,12,128,128]{3,2,1,0:T(8,128)(2,1)} %get-tuple-element.178, s32[1024]{0:T(1024)S(1)} %pad_clamp_fusion.2), kind=kCustom, calls=%fused_computation.2.clone.1 | custom fusion | bytes 2359308 | tf_op jit(solution)/shard_map/while/body/eval_jaxpr/jit(_take)/gather | solution.py:25
  136.3 1.4 fusion.32
  138.4 3.8 %gather_fusion = bf16[3,12,128,128]{3,2,1,0:T(8,128)(2,1)S(1)} fusion(bf16[18,12,128,128]{3,2,1,0:T(8,128)(2,1)} %get-tuple-element.178, s32[1024]{0:T(1024)S(1)} %pad_clamp_fusion.2), kind=kCustom, calls=%fused_computation.2.clone.1 | custom fusion | bytes 2359308 | tf_op jit(solution)/shard_map/while/body/eval_jaxpr/jit(_take)/gather | solution.py:25
  144.7 1.5 fusion.32
  146.9 3.8 %gather_fusion = bf16[3,12,128,128]{3,2,1,0:T(8,128)(2,1)S(1)} fusion(bf16[18,12,128,128]{3,2,1,0:T(8,128)(2,1)} %get-tuple-element.178, s32[1024]{0:T(1024)S(1)} %pad_clamp_fusion.2), kind=kCustom, calls=%fused_computation.2.clone.1 | custom fusion | bytes 2359308 | tf_op jit(solution)/shard_map/while/body/eval_jaxpr/jit(_take)/gather | solution.py:25
  153.2 1.4 fusion.32
  155.3 3.8 %gather_fusion = bf16[3,12,128,128]{3,2,1,0:T(8,128)(2,1)S(1)} fusion(bf16[18,12,128,128]{3,2,1,0:T(8,128)(2,1)} %get-tuple-element.178, s32[1024]{0:T(1024)S(1)} %pad_clamp_fusion.2), kind=kCustom, calls=%fused_computation.2.clone.1 | custom fusion | bytes 2359308 | tf_op jit(solution)/shard_map/while/body/eval_jaxpr/jit(_take)/gather | solution.py:25
  161.6 1.5 fusion.32
  163.8 3.8 %gather_fusion = bf16[3,12,128,128]{3,2,1,0:T(8,128)(2,1)S(1)} fusion(bf16[18,12,128,128]{3,2,1,0:T(8,128)(2,1)} %get-tuple-element.178, s32[1024]{0:T(1024)S(1)} %pad_clamp_fusion.2), kind=kCustom, calls=%fused_computation.2.clone.1 | custom fusion | bytes 2359308 | tf_op jit(solution)/shard_map/while/body/eval_jaxpr/jit(_take)/gather | solution.py:25
  170.1 1.4 fusion.32
  171.6 5.0 %all-to-all-start = ((f32[1,6,12,128,128]{3,4,1,0,2:T(8,128)}), f32[1,6,12,128,128]{3,4,1,0,2:T(8,128)}, u32[]{:S(2)}, u32[]{:S(2)}) async-start(f32[1,6,12,128,128]{3,4,1,0,2:T(8,128)} %bitcast.60), calls=%async_computation | async-start | bytes 9437184 | tf_op jit(solution)/shard_map/all_to_all | solution.py:72
  176.6 3.3 copy.13
  180.0 6.5 %bitcast_convert_fusion = f32[6,128,128]{0,2,1:T(8,128)} fusion(bf16[6,1,128,128]{0,3,2,1:T(8,128)(2,1)} %copy.13), kind=kLoop, calls=%fused_computation.38 | loop fusion | flops 98304 | bytes 589824 | tf_op jit(solution)/shard_map/convert_element_type | solution.py:76
  186.4 1.8 gather_fusion.3
  189.5 42.2 %all-to-all-done = f32[1,6,12,128,128]{3,4,1,0,2:T(8,128)} async-done(((f32[1,6,12,128,128]{3,4,1,0,2:T(8,128)}), f32[1,6,12,128,128]{3,4,1,0,2:T(8,128)}, u32[]{:S(2)}, u32[]{:S(2)}) %all-to-all-start) | async-done | bytes 4718624 | tf_op jit(solution)/shard_map/all_to_all | solution.py:72
  231.6 2.9 reduce_sum.27
  234.6 7.6 %copy.21 = f32[6,1,128,128]{0,3,2,1:T(8,128)} copy(f32[6,1,128,128]{2,3,1,0:T(8,128)S(1)} %copy.33) | data formatting | bytes 786432
  242.2 1.8 gather_fusion.4
  245.3 24.3 %psum.14 = f32[2]{0:T(128)S(1)} all-reduce(f32[2]{0:T(128)S(1)} %pad_maximum_fusion.1), channel_id=1, replica_groups=mesh['row'=16,'col'=8,'fib'=4] {'row'}, use_global_device_ids=true, to_apply=%region_5.6 | all-reduce | flops 2 | bytes 16 | tf_op jit(solution)/shard_map/psum | solution.py:81
  269.7 75.5 %psum.15 = f32[2]{0:T(128)} all-reduce(f32[2]{0:T(128)S(1)} %psum.14), channel_id=1, replica_groups=mesh['row'=16,'col'=8,'fib'=4] {'col','fib'}, use_global_device_ids=true, to_apply=%region_6.7 | all-reduce | flops 2 | bytes 16 | tf_op jit(solution)/shard_map/psum | solution.py:81
  (98 shorter events, 26.9 us)
Async XLA Ops:
  7.2 45.5 %all-gather.2.cloned.1.call-start = ((), (), s32[]{:S(2)}) async-start(), calls=%async_computation.1 | async-start | bytes 2949120 | tf_op jit(solution)/shard_map/all_gather | solution.py:43
  52.7 62.2 %collective-permute-start.4 = (bf16[6,12,128,128]{3,2,1,0:T(8,128)(2,1)}, bf16[6,12,128,128]{3,2,1,0:T(8,128)(2,1)S(1)}, u32[]{:S(2)}, u32[]{:S(2)}) collective-permute-start(bf16[6,12,128,128]{3,2,1,0:T(8,128)(2,1)} %all-gather.2.cloned.1.call-done), channel_id=1, source_target_pairs={{0,4},{4,8},{8,12},{12,16},{16,20},{20,24},{24,28},{28,32},{32,36}... | collective-permute-start | bytes 7077896 | tf_op jit(solution)/shard_map/ppermute | solution.py:16
  56.2 58.7 %collective-permute-start.5 = (bf16[6,12,128,128]{3,2,1,0:T(8,128)(2,1)}, bf16[6,12,128,128]{3,2,1,0:T(8,128)(2,1)}, u32[]{:S(2)}, u32[]{:S(2)}) collective-permute-start(bf16[6,12,128,128]{3,2,1,0:T(8,128)(2,1)} %all-gather.2.cloned.1.call-done), channel_id=1, source_target_pairs={{4,0},{8,4},{12,8},{16,12},{20,16},{24,20},{28,24},{32,28},{36,32}... | collective-permute-start | bytes 7077896 | tf_op jit(solution)/shard_map/ppermute | solution.py:17
  61.6 52.6 %collective-permute-start = (s32[6,12]{1,0:T(8,128)}, s32[6,12]{1,0:T(8,128)S(1)}, u32[]{:S(2)}, u32[]{:S(2)}) collective-permute-start(s32[6,12]{1,0:T(8,128)} %param.6), channel_id=1, source_target_pairs={{0,4},{4,8},{8,12},{12,16},{16,20},{20,24},{24,28},{28,32},{32,36}... | collective-permute-start | bytes 872 | tf_op jit(solution)/shard_map/ppermute | solution.py:16
  63.5 50.7 %collective-permute-start.1 = (s32[6,12]{1,0:T(8,128)}, s32[6,12]{1,0:T(8,128)S(1)}, u32[]{:S(2)}, u32[]{:S(2)}) collective-permute-start(s32[6,12]{1,0:T(8,128)} %param.6), channel_id=1, source_target_pairs={{4,0},{8,4},{12,8},{16,12},{20,16},{24,20},{28,24},{32,28},{36,32}... | collective-permute-start | bytes 872 | tf_op jit(solution)/shard_map/ppermute | solution.py:17
  70.5 36.4 %collective-permute-start.2 = (s32[6]{0:T(128)}, s32[6]{0:T(128)S(1)}, u32[]{:S(2)}, u32[]{:S(2)}) collective-permute-start(s32[6]{0:T(128)} %param.7), channel_id=1, source_target_pairs={{0,4},{4,8},{8,12},{12,16},{16,20},{20,24},{24,28},{28,32},{32,36}... | collective-permute-start | bytes 80 | tf_op jit(solution)/shard_map/ppermute | solution.py:16
  106.9 6.5 %collective-permute-start.3 = (s32[6]{0:T(128)}, s32[6]{0:T(128)S(1)}, u32[]{:S(2)}, u32[]{:S(2)}) collective-permute-start(s32[6]{0:T(128)} %param.7), channel_id=1, source_target_pairs={{4,0},{8,4},{12,8},{16,12},{20,16},{24,20},{28,24},{32,28},{36,32}... | collective-permute-start | bytes 80 | tf_op jit(solution)/shard_map/ppermute | solution.py:17
  114.9 5.9 %copy-start = (bf16[6,3,128,128]{3,2,1,0:T(8,128)(2,1)S(1)}, bf16[6,3,128,128]{3,2,1,0:T(8,128)(2,1)}, u32[]{:S(2)}) copy-start(bf16[6,3,128,128]{3,2,1,0:T(8,128)(2,1)} %param.5) | copy-start | bytes 1769476
  171.6 60.1 %all-to-all-start = ((f32[1,6,12,128,128]{3,4,1,0,2:T(8,128)}), f32[1,6,12,128,128]{3,4,1,0,2:T(8,128)}, u32[]{:S(2)}, u32[]{:S(2)}) async-start(f32[1,6,12,128,128]{3,4,1,0,2:T(8,128)} %bitcast.60), calls=%async_computation | async-start | bytes 9437184 | tf_op jit(solution)/shard_map/all_to_all | solution.py:72
Sparse Core Ops, SparseCore 0:
  10.1 42.5 all-gather.1
